TPU v7x, 32 devices: a whole 2x2x4 slice. The times are simulated.
32 devices in a mesh: section: 2 (over y), tensor: 4 (over z), dp: 4 (over x, core).
Axes of the slice: x: 2, y: 2, z: 4, core: 2. Of those that a mesh axis runs over, the one named last changes fastest.
Arguments:
- tokens_in: bfloat16 [4, 256, 4, 2048], P(None, 'tensor', 'dp'), may hold values from -6 to 6
- cotangent: bfloat16 [4, 256, 4, 2048], P(None, 'tensor', 'dp'), may hold values from -6 to 6
- ln1_gain: bfloat16 [2, 2048], P('section'), may hold values from 0.5 to 1.5
- ln1_bias: bfloat16 [2, 2048], P('section'), may hold values from -1 to 1
- q_weight: bfloat16 [2, 2048, 2048], P('section', None, 'tensor'), may hold values from -0.125 to 0.125
- q_bias: bfloat16 [2, 2048], P('section', 'tensor'), may hold values from -1.5 to 1.5
- kv_weight: bfloat16 [2, 2048, 256], P('section'), may hold values from -0.125 to 0.125
- v_bias: bfloat16 [2, 128], P('section'), may hold values from -0.25 to 0.25
- o_weight: bfloat16 [2, 2048, 2048], P('section', 'tensor'), may hold values from -1.5 to 1.5
- o_bias: bfloat16 [2, 2048], P('section'), may hold values from -1.5 to 1.5
- ln2_gain: bfloat16 [2, 2048], P('section'), may hold values from 0.5 to 1.5
- ln2_bias: bfloat16 [2, 2048], P('section'), may hold values from -1 to 1
- up_weight: bfloat16 [2, 2048, 8192], P('section', None, 'tensor'), may hold values from -0.125 to 0.125
- up_bias: bfloat16 [2, 8192], P('section', 'tensor'), may hold values from -1.5 to 1.5
- down_weight: bfloat16 [2, 8192, 2048], P('section', 'tensor'), may hold values from -0.0625 to 0.0625
- down_bias: bfloat16 [2, 2048], P('section'), may hold values from -1.5 to 1.5
Outputs:
- layer_out: bfloat16 [2, 4, 256, 4, 2048], P('section', None, 'tensor', 'dp')
- input_grad: float32 [2, 4, 256, 4, 2048], P('section', None, 'tensor', 'dp')
- ln1_gain_grad: float32 [2, 2048], P('section')
- ln1_bias_grad: float32 [2, 2048], P('section')
- q_weight_grad: float32 [2, 2048, 2048], P('section', None, 'tensor')
- q_bias_grad: float32 [2, 2048], P('section', 'tensor')
- kv_weight_grad: float32 [2, 2048, 256], P('section')
- v_bias_grad: float32 [2, 128], P('section')
- o_weight_grad: float32 [2, 2048, 2048], P('section', 'tensor')
- o_bias_grad: float32 [2, 2048], P('section')
- ln2_gain_grad: float32 [2, 2048], P('section')
- ln2_bias_grad: float32 [2, 2048], P('section')
- up_weight_grad: float32 [2, 2048, 8192], P('section', None, 'tensor')
- up_bias_grad: float32 [2, 8192], P('section', 'tensor')
- down_weight_grad: float32 [2, 8192, 2048], P('section', 'tensor')
- down_bias_grad: float32 [2, 2048], P('section')
All inputs are finite; a program needn't handle non-finite values.
Results may differ from a plain program's by a relative error of at most 0.022.
Values may be sent and summed in bfloat16 or wider, within the bound.
A program may use at most 512 MiB of HBM per device.

v0:
```python
import math
import jax
import jax.numpy as jnp
from jax import lax
from jax.sharding import PartitionSpec as P

HD = 128
F32 = jnp.float32
BF16 = jnp.bfloat16


def from_behind(block, axis, distance):
    devices = range(lax.axis_size(axis))
    route = [(i - distance, i) for i in devices if i - distance in devices]
    return lax.ppermute(block, axis, route)


def layer_norm(values, gain_vec, bias_vec):
    row_mean = jnp.mean(values, axis=-1, keepdims=True)
    centred = values - row_mean
    row_var = jnp.mean(centred * centred, axis=-1, keepdims=True)
    return centred * lax.rsqrt(row_var + 1e-05) * gain_vec + bias_vec


def gelu_tanh(values):
    return jax.nn.gelu(values, approximate=True)


def dot(a, b):
    return jnp.dot(a, b, preferred_element_type=F32)


def dot_t(a, b):
    return lax.dot_general(a, b, (((1,), (1,)), ((), ())), preferred_element_type=F32)


def t_dot(a, b):
    return lax.dot_general(a, b, (((0,), (0,)), ((), ())), preferred_element_type=F32)


def gather_rows(own_rows):
    return lax.all_gather(own_rows, "tensor", axis=0, tiled=True)


def sum_rows(partial):
    return lax.psum_scatter(partial.astype(BF16), "tensor", scatter_dimension=0, tiled=True).astype(
        F32
    )


def swap(value, distance):
    size = lax.axis_size("dp")
    return lax.ppermute(value, "dp", [(i, i ^ distance) for i in range(size)])


def fold(value, distance, axis):
    bit = lax.axis_index("dp") // distance % 2
    half = value.shape[axis] // 2
    away = lax.dynamic_slice_in_dim(value, (1 - bit) * half, half, axis)
    kept = lax.dynamic_slice_in_dim(value, bit * half, half, axis)
    return kept + swap(away.astype(BF16), distance).astype(F32)


def unfold(value, distance, axis):
    bit = lax.axis_index("dp") // distance % 2
    other = swap(value, distance)
    low = jnp.where(bit == 0, value, other)
    high = jnp.where(bit == 0, other, value)
    return jnp.concatenate([low, high], axis=axis)


def sum_dp(value, axis, scatter=None):
    size = lax.axis_size("dp")
    distance = 1
    while distance < size:
        value = fold(value, distance, axis)
        if distance == 1 and scatter is not None:
            value = lax.psum_scatter(
                value.astype(BF16), "tensor", scatter_dimension=scatter, tiled=True
            ).astype(F32)
        distance *= 2
    value = value.astype(BF16)
    while distance > 1:
        distance //= 2
        value = unfold(value, distance, axis)
    return value.astype(F32)


def whole_weight(shard, split, join):
    size = lax.axis_size("dp")
    part = shard.shape[split] // size
    own = lax.dynamic_slice_in_dim(shard, lax.axis_index("dp") * part, part, split)
    own = lax.all_gather(own, "tensor", axis=join, tiled=True)
    return lax.all_gather(own, "dp", axis=split, tiled=True)


def on_device(
    tokens_in,
    cotangent,
    ln1_gain,
    ln1_bias,
    q_weight,
    q_bias,
    kv_weight,
    v_bias,
    o_weight,
    o_bias,
    ln2_gain,
    ln2_bias,
    up_weight,
    up_bias,
    down_weight,
    down_bias,
):
    section = lax.axis_index("section")
    tensor_count = lax.axis_size("tensor")
    tensor_rank = lax.axis_index("tensor")
    gain_one = ln1_gain[0].astype(F32)
    bias_one = ln1_bias[0].astype(F32)
    w_pairs = kv_weight[0]
    pair_bias = jnp.concatenate([jnp.zeros((HD,), F32), v_bias[0].astype(F32)])
    b_out = o_bias[0].astype(F32)
    gain_two = ln2_gain[0].astype(F32)
    bias_two = ln2_bias[0].astype(F32)
    w_up = up_weight[0]
    b_up = up_bias[0].astype(F32)
    w_down = down_weight[0]
    b_down = down_bias[0].astype(F32)
    blocks, own_count, seq_count, model_dim = tokens_in.shape
    assert seq_count == 1
    tokens_in = tokens_in[:, :, 0]
    cotangent = cotangent[:, :, 0]
    block_len = own_count * tensor_count
    total_len = blocks * block_len
    w_query = whole_weight(q_weight[0], 0, 1)
    w_out = whole_weight(o_weight[0], 1, 0)
    b_query = lax.all_gather(q_bias[0], "tensor", axis=0, tiled=True).astype(F32)
    heads = w_query.shape[1] // HD
    width = heads * HD
    ff_local = w_up.shape[1]
    score_scale = 1.0 / math.sqrt(HD)
    positions = jnp.arange(total_len, dtype=jnp.int32)

    def zeros(shape, dtype):
        return jnp.zeros(shape, dtype)

    kept_normed = zeros((blocks, own_count, model_dim), BF16)
    kept_query = zeros((blocks, own_count, width), BF16)
    kept_attended = zeros((blocks, own_count, width), BF16)
    kept_logsum = zeros((blocks, own_count * heads), F32)
    kv_cache = zeros((total_len, 2 * HD), BF16)
    kept_input = zeros((blocks, own_count, model_dim), F32)
    kept_hidden = zeros((blocks, own_count, model_dim), F32)
    kept_normed_two = zeros((blocks, block_len, model_dim), BF16)
    kept_pre = zeros((blocks, block_len, ff_local), F32)
    kept_active = zeros((blocks, block_len, ff_local), BF16)
    outputs = zeros((blocks, own_count, model_dim), BF16)
    received = zeros((own_count, model_dim), F32)

    def put(kept, value, index):
        return lax.dynamic_update_index_in_dim(kept, value, index, 0)

    def take(kept, index):
        return lax.dynamic_index_in_dim(kept, index, 0, keepdims=False)

    for turn in range(blocks + 1):
        block_index = jnp.clip(turn - section, 0, blocks - 1)
        layer_input = jnp.where(section == 0, take(tokens_in, block_index).astype(F32), received)
        normed = layer_norm(layer_input, gain_one, bias_one).astype(BF16)
        pairs = gather_rows((dot(normed, w_pairs) + pair_bias).astype(BF16))
        kv_cache = lax.dynamic_update_slice_in_dim(kv_cache, pairs, block_index * block_len, 0)
        query = (dot(normed, w_query) + b_query).astype(BF16)
        visible = positions < (block_index + 1) * block_len
        query_rows = query.reshape(own_count * heads, HD)
        scores = dot_t(query_rows, kv_cache[:, :HD]) * score_scale
        scores = jnp.where(visible, scores, -1e30)
        row_top = jnp.max(scores, axis=-1, keepdims=True)
        exponent = jnp.exp(scores - row_top)
        row_total = jnp.sum(exponent, axis=-1, keepdims=True)
        log_total = (row_top + jnp.log(row_total))[:, 0]
        weights_low = (exponent / row_total).astype(BF16)
        attended = dot(weights_low, kv_cache[:, HD:]).astype(BF16).reshape(own_count, width)
        hidden = layer_input + dot(attended, w_out) + b_out
        normed_two = gather_rows(layer_norm(hidden, gain_two, bias_two).astype(BF16))
        pre_active = dot(normed_two, w_up) + b_up
        active = gelu_tanh(pre_active).astype(BF16)
        result_low = (hidden + sum_rows(dot(active, w_down)) + b_down).astype(BF16)
        kept_normed = put(kept_normed, normed, block_index)
        kept_query = put(kept_query, query, block_index)
        kept_attended = put(kept_attended, attended, block_index)
        kept_logsum = put(kept_logsum, log_total, block_index)
        kept_input = put(kept_input, layer_input, block_index)
        kept_hidden = put(kept_hidden, hidden, block_index)
        kept_normed_two = put(kept_normed_two, normed_two, block_index)
        kept_pre = put(kept_pre, pre_active, block_index)
        kept_active = put(kept_active, active, block_index)
        outputs = put(outputs, result_low, block_index)
        if turn < blocks:
            received = from_behind(result_low, "section", 1).astype(F32)
    key_rows = kv_cache[:, :HD]
    value_rows = kv_cache[:, HD:]
    kept_grad_mlp = zeros((blocks + 1, block_len, model_dim), BF16)
    kept_grad_pre = zeros((blocks + 1, block_len, ff_local), BF16)
    kept_branch = zeros((blocks + 1, own_count, model_dim), BF16)
    kept_grad_query = zeros((blocks + 1, own_count, width), BF16)
    kept_grad_pairs = zeros((blocks + 1, own_count, 2 * HD), BF16)
    input_grads = zeros((blocks + 1, own_count, model_dim), F32)
    pair_grad_acc = zeros((total_len, 2 * HD), F32)
    received_back = zeros((own_count, model_dim), F32)
    common = [zeros((model_dim,), F32) for _ in range(6)]
    for turn in range(blocks + 1):
        step_count = turn - (1 - section)
        valid = (step_count >= 0) & (step_count < blocks)
        block_index = blocks - 1 - jnp.clip(step_count, 0, blocks - 1)
        slot = jnp.where(valid, block_index, blocks)
        grad_out = jnp.where(section == 1, take(cotangent, block_index).astype(F32), received_back)
        grad_out = grad_out * valid.astype(F32)
        pre_active = take(kept_pre, block_index)
        grad_mlp = gather_rows(grad_out.astype(BF16))
        grad_active = dot_t(grad_mlp, w_down)
        grad_pre = jax.vjp(gelu_tanh, pre_active)[1](grad_active)[0].astype(BF16)
        grad_normed_two = sum_rows(dot_t(grad_pre, w_up))
        norm_back_two = jax.vjp(layer_norm, take(kept_hidden, block_index), gain_two, bias_two)[1]
        grad_hidden_norm, gain_two_term, bias_two_term = norm_back_two(grad_normed_two)
        grad_hidden = grad_out + grad_hidden_norm
        branch = grad_hidden.astype(BF16)
        grad_attended = dot_t(branch, w_out).astype(BF16).reshape(own_count * heads, HD)
        query_rows = take(kept_query, block_index).reshape(own_count * heads, HD)
        log_total = take(kept_logsum, block_index)
        visible = positions < (block_index + 1) * block_len
        scores = dot_t(query_rows, key_rows) * score_scale
        scores = jnp.where(visible, scores, -1e30)
        probabilities = jnp.exp(scores - log_total[:, None])
        grad_probs = dot_t(grad_attended, value_rows)
        row_inner = jnp.sum(probabilities * grad_probs, axis=-1, keepdims=True)
        grad_scores = (probabilities * (grad_probs - row_inner)).astype(BF16)
        grad_query = (dot(grad_scores, key_rows) * score_scale).astype(BF16)
        grad_query = grad_query.reshape(own_count, width)
        grad_keys = t_dot(grad_scores, query_rows) * score_scale
        grad_values = t_dot(probabilities.astype(BF16), grad_attended)
        pair_grad_acc = pair_grad_acc + jnp.concatenate([grad_keys, grad_values], axis=-1)
        block_pairs = lax.dynamic_slice_in_dim(pair_grad_acc, block_index * block_len, block_len, 0)
        grad_pairs = sum_rows(block_pairs).astype(BF16)
        grad_normed = dot_t(grad_query, w_query) + dot_t(grad_pairs, w_pairs)
        norm_back_one = jax.vjp(layer_norm, take(kept_input, block_index), gain_one, bias_one)[1]
        grad_input_norm, gain_one_term, bias_one_term = norm_back_one(grad_normed)
        grad_input = grad_hidden + grad_input_norm
        if turn < blocks:
            received_back = from_behind(grad_input.astype(BF16), "section", -1).astype(F32)
        scale = valid.astype(F32)
        terms = (
            gain_one_term * scale,
            bias_one_term * scale,
            jnp.sum(grad_hidden, axis=0),
            gain_two_term,
            bias_two_term,
            jnp.sum(grad_out, axis=0),
        )
        common = [total + term for total, term in zip(common, terms)]
        input_grads = put(input_grads, grad_input, slot)
        kept_grad_mlp = put(kept_grad_mlp, grad_mlp, slot)
        kept_grad_pre = put(kept_grad_pre, grad_pre, slot)
        kept_branch = put(kept_branch, branch, slot)
        kept_grad_query = put(kept_grad_query, grad_query, slot)
        kept_grad_pairs = put(kept_grad_pairs, grad_pairs, slot)

    def flat(kept):
        return kept[:blocks].reshape(-1, kept.shape[-1])

    down_w = t_dot(flat(kept_active), flat(kept_grad_mlp))
    up_w = t_dot(flat(kept_normed_two), flat(kept_grad_pre))
    up_b = jnp.sum(flat(kept_grad_pre).astype(F32), axis=0)
    out_w = t_dot(flat(kept_attended), flat(kept_branch))
    query_w = t_dot(flat(kept_normed), flat(kept_grad_query))
    query_b = jnp.sum(flat(kept_grad_query).astype(F32), axis=0)
    pair_w = t_dot(flat(kept_normed), flat(kept_grad_pairs))
    value_b = jnp.sum(flat(kept_grad_pairs)[:, HD:].astype(F32), axis=0)
    down_w = sum_dp(down_w, 0)
    up_w = sum_dp(up_w, 0)
    out_w = sum_dp(out_w, 1, 0)
    query_w = sum_dp(query_w, 0, 1)
    pair_w = lax.psum(pair_w.astype(BF16), ("tensor", "dp")).astype(F32)
    wide = jnp.zeros((tensor_count, ff_local), F32)
    wide = lax.dynamic_update_index_in_dim(wide, up_b, tensor_rank, 0)
    packed = jnp.concatenate([*common, query_b, value_b, wide.reshape(-1)])
    packed = lax.psum(packed, ("tensor", "dp"))
    vecs = packed[: 6 * model_dim].reshape(6, model_dim)
    own_query = lax.dynamic_slice_in_dim(
        packed, 6 * model_dim + tensor_rank * (width // tensor_count), width // tensor_count, 0
    )
    value_b = lax.slice_in_dim(packed, 6 * model_dim + width, 6 * model_dim + width + HD)
    own_up = lax.dynamic_slice_in_dim(
        packed, 6 * model_dim + width + HD + tensor_rank * ff_local, ff_local, 0
    )
    return (
        outputs[None, :, :, None],
        input_grads[None, :blocks, :, None],
        vecs[0][None],
        vecs[1][None],
        query_w[None],
        own_query[None],
        pair_w[None],
        value_b[None],
        out_w[None],
        vecs[2][None],
        vecs[3][None],
        vecs[4][None],
        up_w[None],
        own_up[None],
        down_w[None],
        vecs[5][None],
    )


def solution(mesh):
    placed = (
        P(None, "tensor", "dp", None),
        P(None, "tensor", "dp", None),
        P("section", None),
        P("section", None),
        P("section", None, "tensor"),
        P("section", "tensor"),
        P("section", None, None),
        P("section", None),
        P("section", "tensor", None),
        P("section", None),
        P("section", None),
        P("section", None),
        P("section", None, "tensor"),
        P("section", "tensor"),
        P("section", "tensor", None),
        P("section", None),
    )
    return jax.shard_map(
        on_device,
        mesh=mesh,
        in_specs=placed,
        out_specs=(
            P("section", None, "tensor", "dp", None),
            P("section", None, "tensor", "dp", None),
            P("section", None),
            P("section", None),
            P("section", None, "tensor"),
            P("section", "tensor"),
            P("section", None, None),
            P("section", None),
            P("section", "tensor", None),
            P("section", None),
            P("section", None),
            P("section", None),
            P("section", None, "tensor"),
            P("section", "tensor"),
            P("section", "tensor", None),
            P("section", None),
        ),
        check_vma=False,
    )
```

profile of v0, /device:TPU:1, one launch (start us, length us, event | category | flops | bytes accessed | tf_op | source)
XLA Modules:
  0.0 1809.0 jit_solution(15878004784130863771)
XLA Ops:
  11.7 46.6 %all-gather.40.cloned.1.call-done = bf16[1,512,2048]{2,1,0:T(8,128)(2,1)} async-done(((bf16[1,512,512]{2,1,0:T(8,128)(2,1)}), bf16[1,512,2048]{2,1,0:T(8,128)(2,1)}) %all-gather.40.cloned.1.call-update) | async-done | bytes 2097168 | tf_op jit(solution)/shard_map/all_gather | solution.py:93
  58.3 46.8 %all-gather.44.cloned.1.call-done = bf16[1,2048,512]{2,1,0:T(8,128)(2,1)} async-done(((bf16[1,512,512]{2,1,0:T(8,128)(2,1)}), bf16[1,2048,512]{2,1,0:T(8,128)(2,1)}) %all-gather.44.cloned.1.call-update) | async-done | bytes 2097168 | tf_op jit(solution)/shard_map/all_gather | solution.py:93
  105.3 9.3 all-gather.2
  115.5 11.1 all_gather.63
  126.7 37.5 %all-gather.42.cloned.1.call-done = bf16[1,2048,2048]{2,1,0:T(8,128)(2,1)} async-done(((bf16[1,512,2048]{2,1,0:T(8,128)(2,1)}), bf16[1,2048,2048]{2,1,0:T(8,128)(2,1)}) %all-gather.42.cloned.1.call-update) | async-done | bytes 8388624 | tf_op jit(solution)/shard_map/all_gather | solution.py:94
  174.8 49.1 %all-gather.46.cloned.1.call-done = bf16[1,2048,2048]{2,1,0:T(8,128)(2,1)} async-done(((bf16[1,2048,512]{2,1,0:T(8,128)(2,1)}), bf16[1,2048,2048]{2,1,0:T(8,128)(2,1)}) %all-gather.46.cloned.1.call-update) | async-done | bytes 8388624 | tf_op jit(solution)/shard_map/all_gather | solution.py:94
  230.4 27.2 %all-gather.20.cloned.1.call-done = bf16[256,2048]{1,0:T(8,128)(2,1)} async-done(((bf16[64,2048]{1,0:T(8,128)(2,1)}), bf16[256,2048]{1,0:T(8,128)(2,1)}) %all-gather.20.cloned.1.call-update) | async-done | bytes 1048592 | tf_op jit(solution)/shard_map/all_gather | solution.py:42
  262.1 7.2 bitcast_dynamic-update-slice_fusion.4
  274.3 26.7 %reduce-scatter.18.cloned.1.call-done = bf16[64,2048]{1,0:T(8,128)(2,1)} async-done(((bf16[256,2048]{1,0:T(8,128)(2,1)}), bf16[64,2048]{1,0:T(8,128)(2,1)}) %reduce-scatter.18.cloned.1.call-update) | async-done | bytes 262160 | tf_op jit(solution)/shard_map/reduce_scatter | solution.py:46
  312.8 11.2 all_gather.67
  342.7 30.8 %all-gather.22.cloned.1.call-done = bf16[256,2048]{1,0:T(8,128)(2,1)} async-done(((bf16[64,2048]{1,0:T(8,128)(2,1)}), bf16[256,2048]{1,0:T(8,128)(2,1)}) %all-gather.22.cloned.1.call-update) | async-done | bytes 1048592 | tf_op jit(solution)/shard_map/all_gather | solution.py:42
  373.4 7.4 bitcast_dynamic-update-slice_fusion.3
  389.1 26.7 %reduce-scatter.20.cloned.1.call-done = bf16[64,2048]{1,0:T(8,128)(2,1)} async-done(((bf16[256,2048]{1,0:T(8,128)(2,1)}), bf16[64,2048]{1,0:T(8,128)(2,1)}) %reduce-scatter.20.cloned.1.call-update) | async-done | bytes 262160 | tf_op jit(solution)/shard_map/reduce_scatter | solution.py:46
  426.6 11.2 all_gather.69
  456.2 31.1 %all-gather.24.cloned.1.call-done = bf16[256,2048]{1,0:T(8,128)(2,1)} async-done(((bf16[64,2048]{1,0:T(8,128)(2,1)}), bf16[256,2048]{1,0:T(8,128)(2,1)}) %all-gather.24.cloned.1.call-update) | async-done | bytes 1048592 | tf_op jit(solution)/shard_map/all_gather | solution.py:42
  487.3 7.4 bitcast_dynamic-update-slice_fusion.2
  502.9 26.7 %reduce-scatter.22.cloned.1.call-done = bf16[64,2048]{1,0:T(8,128)(2,1)} async-done(((bf16[256,2048]{1,0:T(8,128)(2,1)}), bf16[64,2048]{1,0:T(8,128)(2,1)}) %reduce-scatter.22.cloned.1.call-update) | async-done | bytes 262160 | tf_op jit(solution)/shard_map/reduce_scatter | solution.py:46
  540.4 11.2 all_gather.71
  570.0 31.0 %all-gather.26.cloned.1.call-done = bf16[256,2048]{1,0:T(8,128)(2,1)} async-done(((bf16[64,2048]{1,0:T(8,128)(2,1)}), bf16[256,2048]{1,0:T(8,128)(2,1)}) %all-gather.26.cloned.1.call-update) | async-done | bytes 1048592 | tf_op jit(solution)/shard_map/all_gather | solution.py:42
  601.1 7.4 bitcast_dynamic-update-slice_fusion.1
  616.7 26.7 %reduce-scatter.24.cloned.1.call-done = bf16[64,2048]{1,0:T(8,128)(2,1)} async-done(((bf16[256,2048]{1,0:T(8,128)(2,1)}), bf16[64,2048]{1,0:T(8,128)(2,1)}) %reduce-scatter.24.cloned.1.call-update) | async-done | bytes 262160 | tf_op jit(solution)/shard_map/reduce_scatter | solution.py:46
  654.3 10.5 all_gather.73
  702.6 9.3 all-gather.28.cloned.1.call-done
  711.8 8.1 bitcast_dynamic-update-slice_fusion
  719.9 20.8 %all-gather.30.cloned.1.call-done = bf16[256,2048]{1,0:T(8,128)(2,1)} async-done(((bf16[64,2048]{1,0:T(8,128)(2,1)}), bf16[256,2048]{1,0:T(8,128)(2,1)}) %all-gather.30.cloned.1.call-update) | async-done | bytes 1048592 | tf_op jit(solution)/shard_map/all_gather | solution.py:42
  744.0 8.5 bitcast_dynamic-update-slice_fusion.14
  762.3 20.4 %reduce-scatter.28.cloned.1.call-done = bf16[64,2048]{1,0:T(8,128)(2,1)} async-done(((bf16[256,2048]{1,0:T(8,128)(2,1)}), bf16[64,2048]{1,0:T(8,128)(2,1)}) %reduce-scatter.28.cloned.1.call-update) | async-done | bytes 262160 | tf_op jit(solution)/shard_map/reduce_scatter | solution.py:46
  840.3 28.2 %all-gather.32.cloned.1.call-done = bf16[256,2048]{1,0:T(8,128)(2,1)} async-done(((bf16[64,2048]{1,0:T(8,128)(2,1)}), bf16[256,2048]{1,0:T(8,128)(2,1)}) %all-gather.32.cloned.1.call-update) | async-done | bytes 1048592 | tf_op jit(solution)/shard_map/all_gather | solution.py:42
  868.5 8.6 bitcast_dynamic-update-slice_fusion.13
  889.5 21.2 %reduce-scatter.32.cloned.1.call-done = bf16[64,2048]{1,0:T(8,128)(2,1)} async-done(((bf16[256,2048]{1,0:T(8,128)(2,1)}), bf16[64,2048]{1,0:T(8,128)(2,1)}) %reduce-scatter.32.cloned.1.call-update) | async-done | bytes 262160 | tf_op jit(solution)/shard_map/reduce_scatter | solution.py:46
  967.2 28.4 %all-gather.34.cloned.1.call-done = bf16[256,2048]{1,0:T(8,128)(2,1)} async-done(((bf16[64,2048]{1,0:T(8,128)(2,1)}), bf16[256,2048]{1,0:T(8,128)(2,1)}) %all-gather.34.cloned.1.call-update) | async-done | bytes 1048592 | tf_op jit(solution)/shard_map/all_gather | solution.py:42
  995.6 8.6 bitcast_dynamic-update-slice_fusion.12
  1016.6 21.2 %reduce-scatter.36.cloned.1.call-done = bf16[64,2048]{1,0:T(8,128)(2,1)} async-done(((bf16[256,2048]{1,0:T(8,128)(2,1)}), bf16[64,2048]{1,0:T(8,128)(2,1)}) %reduce-scatter.36.cloned.1.call-update) | async-done | bytes 262160 | tf_op jit(solution)/shard_map/reduce_scatter | solution.py:46
  1122.7 8.6 bitcast_dynamic-update-slice_fusion.11
  1240.0 10.0 all-gather.38.cloned.1.call-done
  1250.0 8.6 bitcast_dynamic-update-slice_fusion.10
  1347.3 18.3 %convolution_bitcast_fusion = f32[2048,2048]{1,0:T(8,128)} fusion(bf16[4,256,2048]{1,2,0:T(8,128)(2,1)} %get-tuple-element.221, bf16[5,256,2048]{2,1,0:T(8,128)(2,1)} %bitcast_dynamic-update-slice_fusion.5), kind=kOutput, calls=%fused_computation | convolution fusion | flops 8589934592 | bytes 25165824 | tf_op jit(solution)/shard_map/dot_general | solution.py:38
  1398.4 8.4 add_convert_fusion.1
  1406.9 12.6 convolution_bitcast_fusion.1
  1464.0 41.4 %collective-permute-done.21 = bf16[512,2048]{1,0:T(8,128)(2,1)} collective-permute-done((bf16[512,2048]{1,0:T(8,128)(2,1)}, bf16[512,2048]{1,0:T(8,128)(2,1)}, u32[]{:S(2)}, u32[]{:S(2)}) %collective-permute-start.21) | collective-permute-done | bytes 2097184 | tf_op jit(solution)/shard_map/ppermute | solution.py:53
  1511.4 8.3 add_convert_fusion
  1522.4 29.8 %collective-permute-done.17 = bf16[512,2048]{1,0:T(8,128)(2,1)} collective-permute-done((bf16[512,2048]{1,0:T(8,128)(2,1)}, bf16[512,2048]{1,0:T(8,128)(2,1)}, u32[]{:S(2)}, u32[]{:S(2)}) %collective-permute-start.17) | collective-permute-done | bytes 2097184 | tf_op jit(solution)/shard_map/ppermute | solution.py:53
  1557.1 43.0 %collective-permute-done.22 = bf16[512,2048]{1,0:T(8,128)(2,1)} collective-permute-done((bf16[512,2048]{1,0:T(8,128)(2,1)}, bf16[512,2048]{1,0:T(8,128)(2,1)}, u32[]{:S(2)}, u32[]{:S(2)}) %collective-permute-start.22) | collective-permute-done | bytes 2097184 | tf_op jit(solution)/shard_map/ppermute | solution.py:53
  1608.0 37.0 %collective-permute-done.18 = bf16[512,2048]{1,0:T(8,128)(2,1)S(1)} collective-permute-done((bf16[512,2048]{1,0:T(8,128)(2,1)S(1)}, bf16[512,2048]{1,0:T(8,128)(2,1)S(1)}, u32[]{:S(2)}, u32[]{:S(2)}) %collective-permute-start.18) | collective-permute-done | bytes 2097184 | tf_op jit(solution)/shard_map/ppermute | solution.py:53
  1669.2 68.0 %reduce-scatter.50.cloned.1.call-done = bf16[512,1024]{1,0:T(8,128)(2,1)} async-done(((bf16[2048,1024]{1,0:T(8,128)(2,1)}), bf16[512,1024]{1,0:T(8,128)(2,1)}) %reduce-scatter.50.cloned.1.call-update) | async-done | bytes 1048592 | tf_op jit(solution)/shard_map/reduce_scatter | solution.py:78
  1740.8 11.8 maximum_convert_fusion.1
  1770.3 7.8 collective-permute-done.14
  1781.1 11.8 maximum_convert_fusion
  (882 shorter events, 781.7 us)
Async XLA Ops:
  7.3 51.0 %all-gather.40.cloned.1.call-start = ((), (), s32[]{:S(2)}) async-start(), calls=%async_computation.46 | async-start | bytes 2621440 | tf_op jit(solution)/shard_map/all_gather | solution.py:93
  9.6 95.5 %all-gather.44.cloned.1.call-start = ((), (), s32[]{:S(2)}) async-start(), calls=%async_computation.48 | async-start | bytes 2621440 | tf_op jit(solution)/shard_map/all_gather | solution.py:93
  11.7 152.5 %all-gather.42.cloned.1.call-start = ((), (), s32[]{:S(2)}) async-start(), calls=%async_computation.47 | async-start | bytes 10485760 | tf_op jit(solution)/shard_map/all_gather | solution.py:94
  58.3 165.6 %all-gather.46.cloned.1.call-start = ((), (), s32[]{:S(2)}) async-start(), calls=%async_computation.49 | async-start | bytes 10485760 | tf_op jit(solution)/shard_map/all_gather | solution.py:94
  105.2 152.5 %all-gather.20.cloned.1.call-start = ((), (), s32[]{:S(2)}) async-start(), calls=%async_computation.17 | async-start | bytes 1310720 | tf_op jit(solution)/shard_map/all_gather | solution.py:42
  230.1 70.8 %reduce-scatter.18.cloned.1.call-start = ((), (), s32[]{:S(2)}) async-start(), calls=%async_computation.18 | async-start | bytes 1310720 | tf_op jit(solution)/shard_map/reduce_scatter | solution.py:46
  274.2 99.2 %all-gather.22.cloned.1.call-start = ((), (), s32[]{:S(2)}) async-start(), calls=%async_computation.19 | async-start | bytes 1310720 | tf_op jit(solution)/shard_map/all_gather | solution.py:42
  342.2 73.6 %reduce-scatter.20.cloned.1.call-start = ((), (), s32[]{:S(2)}) async-start(), calls=%async_computation.20 | async-start | bytes 1310720 | tf_op jit(solution)/shard_map/reduce_scatter | solution.py:46
  389.0 98.2 %all-gather.24.cloned.1.call-start = ((), (), s32[]{:S(2)}) async-start(), calls=%async_computation.21 | async-start | bytes 1310720 | tf_op jit(solution)/shard_map/all_gather | solution.py:42
  456.0 73.7 %reduce-scatter.22.cloned.1.call-start = ((), (), s32[]{:S(2)}) async-start(), calls=%async_computation.22 | async-start | bytes 1310720 | tf_op jit(solution)/shard_map/reduce_scatter | solution.py:46
  502.9 98.2 %all-gather.26.cloned.1.call-start = ((), (), s32[]{:S(2)}) async-start(), calls=%async_computation.23 | async-start | bytes 1310720 | tf_op jit(solution)/shard_map/all_gather | solution.py:42
  569.8 73.7 %reduce-scatter.24.cloned.1.call-start = ((), (), s32[]{:S(2)}) async-start(), calls=%async_computation.24 | async-start | bytes 1310720 | tf_op jit(solution)/shard_map/reduce_scatter | solution.py:46
  616.7 95.2 %all-gather.28.cloned.1.call-start = ((), (), s32[]{:S(2)}) async-start(), calls=%async_computation.25 | async-start | bytes 1310720 | tf_op jit(solution)/shard_map/all_gather | solution.py:42
  680.6 60.1 %all-gather.30.cloned.1.call-start = ((), (), s32[]{:S(2)}) async-start(), calls=%async_computation.27 | async-start | bytes 1310720 | tf_op jit(solution)/shard_map/all_gather | solution.py:42
  683.0 99.7 %reduce-scatter.28.cloned.1.call-start = ((), (), s32[]{:S(2)}) async-start(), calls=%async_computation.28 | async-start | bytes 1310720 | tf_op jit(solution)/shard_map/reduce_scatter | solution.py:46
  755.9 68.3 %reduce-scatter.30.cloned.1.call-start = ((), (), s32[]{:S(2)}) async-start(), calls=%async_computation.29 | async-start | bytes 163840 | tf_op jit(solution)/shard_map/reduce_scatter | solution.py:46
  808.3 60.2 %all-gather.32.cloned.1.call-start = ((), (), s32[]{:S(2)}) async-start(), calls=%async_computation.30 | async-start | bytes 1310720 | tf_op jit(solution)/shard_map/all_gather | solution.py:42
  839.8 70.8 %reduce-scatter.32.cloned.1.call-start = ((), (), s32[]{:S(2)}) async-start(), calls=%async_computation.31 | async-start | bytes 1310720 | tf_op jit(solution)/shard_map/reduce_scatter | solution.py:46
  883.9 68.3 %reduce-scatter.34.cloned.1.call-start = ((), (), s32[]{:S(2)}) async-start(), calls=%async_computation.32 | async-start | bytes 163840 | tf_op jit(solution)/shard_map/reduce_scatter | solution.py:46
  936.3 59.3 %all-gather.34.cloned.1.call-start = ((), (), s32[]{:S(2)}) async-start(), calls=%async_computation.33 | async-start | bytes 1310720 | tf_op jit(solution)/shard_map/all_gather | solution.py:42
  967.0 70.8 %reduce-scatter.36.cloned.1.call-start = ((), (), s32[]{:S(2)}) async-start(), calls=%async_computation.34 | async-start | bytes 1310720 | tf_op jit(solution)/shard_map/reduce_scatter | solution.py:46
  1011.0 68.3 %reduce-scatter.38.cloned.1.call-start = ((), (), s32[]{:S(2)}) async-start(), calls=%async_computation.35 | async-start | bytes 163840 | tf_op jit(solution)/shard_map/reduce_scatter | solution.py:46
  1063.4 59.3 %all-gather.36.cloned.1.call-start = ((), (), s32[]{:S(2)}) async-start(), calls=%async_computation.36 | async-start | bytes 1310720 | tf_op jit(solution)/shard_map/all_gather | solution.py:42
  1094.1 70.8 %reduce-scatter.40.cloned.1.call-start = ((), (), s32[]{:S(2)}) async-start(), calls=%async_computation.37 | async-start | bytes 1310720 | tf_op jit(solution)/shard_map/reduce_scatter | solution.py:46
  1138.1 68.3 %reduce-scatter.42.cloned.1.call-start = ((), (), s32[]{:S(2)}) async-start(), calls=%async_computation.38 | async-start | bytes 163840 | tf_op jit(solution)/shard_map/reduce_scatter | solution.py:46
  1190.6 59.4 %all-gather.38.cloned.1.call-start = ((), (), s32[]{:S(2)}) async-start(), calls=%async_computation.39 | async-start | bytes 1310720 | tf_op jit(solution)/shard_map/all_gather | solution.py:42
  1221.3 70.8 %reduce-scatter.44.cloned.1.call-start = ((), (), s32[]{:S(2)}) async-start(), calls=%async_computation.40 | async-start | bytes 1310720 | tf_op jit(solution)/shard_map/reduce_scatter | solution.py:46
  1265.4 118.9 %reduce-scatter.46.cloned.1.call-start = ((), (), s32[]{:S(2)}) async-start(), calls=%async_computation.41 | async-start | bytes 163840 | tf_op jit(solution)/shard_map/reduce_scatter | solution.py:46
  1314.2 205.5 %reduce-scatter.26.cloned.1.call-start = ((), (), s32[]{:S(2)}) async-start(), calls=%async_computation.26 | async-start | bytes 1310720 | tf_op jit(solution)/shard_map/reduce_scatter | solution.py:46
  1321.3 331.7 %all-reduce.4.cloned.1.call-start = ((), (), s32[]{:S(2)}) async-start(), calls=%async_computation.42 | async-start | bytes 188416 | tf_op jit(solution)/shard_map/psum | solution.py:286
  1346.4 52.0 %collective-permute-start.8 = (bf16[1024,2048]{1,0:T(8,128)(2,1)}, bf16[1024,2048]{1,0:T(8,128)(2,1)}, u32[]{:S(2)}, u32[]{:S(2)}) collective-permute-start(bf16[1024,2048]{1,0:T(8,128)(2,1)} %dynamic-slice_convert_fusion.3), channel_id=1, source_target_pairs={{0,1},{1,0},{2,3},{3,2},{4,5},{5,4},{6,7},{7,6},{8,9},{9,8},{10,11... | collective-permute-start | bytes 12582920 | tf_op jit(solution)/shard_map/ppermute | solution.py:53
  1374.7 69.2 %collective-permute-start.20 = (bf16[1024,2048]{1,0:T(8,128)(2,1)}, bf16[1024,2048]{1,0:T(8,128)(2,1)}, u32[]{:S(2)}, u32[]{:S(2)}) collective-permute-start(bf16[1024,2048]{1,0:T(8,128)(2,1)} %dynamic-slice_convert_fusion), channel_id=1, source_target_pairs={{0,1},{1,0},{2,3},{3,2},{4,5},{5,4},{6,7},{7,6},{8,9},{9,8},{10,11... | collective-permute-start | bytes 12582920 | tf_op jit(solution)/shard_map/ppermute | solution.py:53
  1395.6 261.4 %all-reduce.6.cloned.1.call-start = ((), (), s32[]{:S(2)}) async-start(), calls=%async_computation.44 | async-start | bytes 2097152 | tf_op jit(solution)/shard_map/psum | solution.py:282
  1398.3 267.7 %reduce-scatter.48.cloned.1.call-start = ((), (), s32[]{:S(2)}) async-start(), calls=%async_computation.43 | async-start | bytes 5242880 | tf_op jit(solution)/shard_map/reduce_scatter | solution.py:78
  1406.8 330.3 %reduce-scatter.50.cloned.1.call-start = ((), (), s32[]{:S(2)}) async-start(), calls=%async_computation.45 | async-start | bytes 5242880 | tf_op jit(solution)/shard_map/reduce_scatter | solution.py:78
  1428.2 27.6 %collective-permute-start.16 = (bf16[1024,2048]{1,0:T(8,128)(2,1)}, bf16[1024,2048]{1,0:T(8,128)(2,1)}, u32[]{:S(2)}, u32[]{:S(2)}) collective-permute-start(bf16[1024,2048]{1,0:T(8,128)(2,1)} %dynamic-slice_convert_fusion.1), channel_id=1, source_target_pairs={{0,1},{1,0},{2,3},{3,2},{4,5},{5,4},{6,7},{7,6},{8,9},{9,8},{10,11... | collective-permute-start | bytes 12582920 | tf_op jit(solution)/shard_map/ppermute | solution.py:53
  1443.4 68.0 %collective-permute-start.12 = (bf16[2048,1024]{1,0:T(8,128)(2,1)}, bf16[2048,1024]{1,0:T(8,128)(2,1)}, u32[]{:S(2)}, u32[]{:S(2)}) collective-permute-start(bf16[2048,1024]{1,0:T(8,128)(2,1)} %dynamic-slice_convert_fusion.2), channel_id=1, source_target_pairs={{0,1},{1,0},{2,3},{3,2},{4,5},{5,4},{6,7},{7,6},{8,9},{9,8},{10,11... | collective-permute-start | bytes 12582920 | tf_op jit(solution)/shard_map/ppermute | solution.py:53
  1454.7 50.7 %collective-permute-start.21 = (bf16[512,2048]{1,0:T(8,128)(2,1)}, bf16[512,2048]{1,0:T(8,128)(2,1)}, u32[]{:S(2)}, u32[]{:S(2)}) collective-permute-start(bf16[512,2048]{1,0:T(8,128)(2,1)} %dynamic-slice_convert_fusion.4), channel_id=1, source_target_pairs={{0,2},{1,3},{2,0},{3,1},{4,6},{5,7},{6,4},{7,5},{8,10},{9,11},{10,... | collective-permute-start | bytes 6291464 | tf_op jit(solution)/shard_map/ppermute | solution.py:53
  1463.7 88.6 %collective-permute-start.17 = (bf16[512,2048]{1,0:T(8,128)(2,1)}, bf16[512,2048]{1,0:T(8,128)(2,1)}, u32[]{:S(2)}, u32[]{:S(2)}) collective-permute-start(bf16[512,2048]{1,0:T(8,128)(2,1)} %dynamic-slice_convert_fusion.5), channel_id=1, source_target_pairs={{0,2},{1,3},{2,0},{3,1},{4,6},{5,7},{6,4},{7,5},{8,10},{9,11},{10,... | collective-permute-start | bytes 6291464 | tf_op jit(solution)/shard_map/ppermute | solution.py:53
  1510.3 89.7 %collective-permute-start.22 = (bf16[512,2048]{1,0:T(8,128)(2,1)}, bf16[512,2048]{1,0:T(8,128)(2,1)}, u32[]{:S(2)}, u32[]{:S(2)}) collective-permute-start(bf16[512,2048]{1,0:T(8,128)(2,1)} %add_convert_fusion.2), channel_id=1, source_target_pairs={{0,2},{1,3},{2,0},{3,1},{4,6},{5,7},{6,4},{7,5},{8,10},{9,11},{10,... | collective-permute-start | bytes 6291464 | tf_op jit(solution)/shard_map/ppermute | solution.py:53
  1555.9 89.1 %collective-permute-start.18 = (bf16[512,2048]{1,0:T(8,128)(2,1)S(1)}, bf16[512,2048]{1,0:T(8,128)(2,1)S(1)}, u32[]{:S(2)}, u32[]{:S(2)}) collective-permute-start(bf16[512,2048]{1,0:T(8,128)(2,1)S(1)} %add_convert_fusion.3), channel_id=1, source_target_pairs={{0,2},{1,3},{2,0},{3,1},{4,6},{5,7},{6,4},{7,5},{8,10},{9,11},{10,... | collective-permute-start | bytes 6291464 | tf_op jit(solution)/shard_map/ppermute | solution.py:53
  1606.0 53.9 %collective-permute-start.23 = (bf16[1024,2048]{1,0:T(8,128)(2,1)}, bf16[1024,2048]{1,0:T(8,128)(2,1)}, u32[]{:S(2)}, u32[]{:S(2)}) collective-permute-start(bf16[1024,2048]{1,0:T(8,128)(2,1)} %pad_maximum_fusion.1), channel_id=1, source_target_pairs={{0,1},{1,0},{2,3},{3,2},{4,5},{5,4},{6,7},{7,6},{8,9},{9,8},{10,11... | collective-permute-start | bytes 12582920 | tf_op jit(solution)/shard_map/ppermute | solution.py:53
  1648.8 108.6 %collective-permute-start.19 = (bf16[1024,2048]{1,0:T(8,128)(2,1)}, bf16[1024,2048]{1,0:T(8,128)(2,1)}, u32[]{:S(2)}, u32[]{:S(2)}) collective-permute-start(bf16[1024,2048]{1,0:T(8,128)(2,1)} %pad_maximum_fusion), channel_id=1, source_target_pairs={{0,1},{1,0},{2,3},{3,2},{4,5},{5,4},{6,7},{7,6},{8,9},{9,8},{10,11... | collective-permute-start | bytes 12582920 | tf_op jit(solution)/shard_map/ppermute | solution.py:53
  1667.9 84.7 %collective-permute-start.9 = (bf16[512,512]{1,0:T(8,128)(2,1)S(1)}, bf16[512,512]{1,0:T(8,128)(2,1)S(1)}, u32[]{:S(2)}, u32[]{:S(2)}) collective-permute-start(bf16[512,512]{1,0:T(8,128)(2,1)S(1)} %dynamic-slice_convert_fusion.7), channel_id=1, source_target_pairs={{0,2},{1,3},{2,0},{3,1},{4,6},{5,7},{6,4},{7,5},{8,10},{9,11},{10,... | collective-permute-start | bytes 1572872 | tf_op jit(solution)/shard_map/ppermute | solution.py:53
  1739.6 15.2 collective-permute-start.13
  1756.3 21.7 %collective-permute-start.14 = (bf16[512,512]{1,0:T(8,128)(2,1)S(1)}, bf16[512,512]{1,0:T(8,128)(2,1)S(1)}, u32[]{:S(2)}, u32[]{:S(2)}) collective-permute-start(bf16[512,512]{1,0:T(8,128)(2,1)S(1)} %add_convert_fusion.4), channel_id=1, source_target_pairs={{0,2},{1,3},{2,0},{3,1},{4,6},{5,7},{6,4},{7,5},{8,10},{9,11},{10,... | collective-permute-start | bytes 1572872 | tf_op jit(solution)/shard_map/ppermute | solution.py:53
  1767.0 26.0 %collective-permute-start.11 = (bf16[1024,512]{1,0:T(8,128)(2,1)S(1)}, bf16[1024,512]{1,0:T(8,128)(2,1)}, u32[]{:S(2)}, u32[]{:S(2)}) collective-permute-start(bf16[1024,512]{1,0:T(8,128)(2,1)S(1)} %pad_maximum_fusion.3), channel_id=1, source_target_pairs={{0,1},{1,0},{2,3},{3,2},{4,5},{5,4},{6,7},{7,6},{8,9},{9,8},{10,11... | collective-permute-start | bytes 3145736 | tf_op jit(solution)/shard_map/ppermute | solution.py:53
  1779.3 17.9 collective-permute-start.15
  (182 other events, 3036.3 us)
Sparse Core Ops, SparseCore 0:
  10.3 47.9 all-gather.39
  60.4 44.6 all-gather.43
  106.7 57.4 all-gather.41
  165.6 58.2 all-gather.45
  230.3 27.3 all-gather.19
  274.3 26.6 reduce-scatter.17
  342.3 31.0 all-gather.21
  389.1 26.5 reduce-scatter.19
  456.1 31.1 all-gather.23
  503.0 26.6 reduce-scatter.21
  569.9 31.1 all-gather.25
  616.8 26.5 reduce-scatter.23
  680.7 31.0 all-gather.27
  713.3 27.4 all-gather.29
  756.1 26.6 reduce-scatter.27
  808.5 15.7 reduce-scatter.29
  840.0 28.5 all-gather.31
  884.0 26.6 reduce-scatter.31
  936.5 15.6 reduce-scatter.33
  967.1 28.4 all-gather.33
  1011.1 26.6 reduce-scatter.35
  1063.5 15.7 reduce-scatter.37
  1094.2 28.5 all-gather.35
  1138.2 26.6 reduce-scatter.39
  1190.7 15.6 reduce-scatter.41
  1221.4 28.5 all-gather.37
  1265.5 26.6 reduce-scatter.43
  1314.3 15.6 reduce-scatter.45
  1332.3 27.4 reduce-scatter.25
  1395.7 84.6 all-reduce.3
  1483.8 93.2 all-reduce.5
  1580.0 76.9 reduce-scatter.47
  1659.8 77.2 reduce-scatter.49
where the time goes:
time: 1820 us; the launch traced here: 1810 us
  waiting for transfers between devices  880 us (48%)
  matrix products  387 us (21%)
  other arithmetic  224 us (12%)
  local copies, waits for them, and re-layouts  197 us (11%)
  blocking collectives  64.5 us (4%)
  starting transfers between devices  38.8 us (2%)
    all_gather x10, waiting for transfers between devices, gather_rows(): return lax.all_gather(own_rows, 'tensor', axis=0, tiled=True)  222 us
    reduce_scatter x15, waiting for transfers between devices, sum_rows(): lax.psum_scatter(partial.astype(BF16), 'tensor', scatter_dimension=0, til...  205 us
    dot_general x40, matrix products, dot_t(): lax.dot_general(a, b, (((1,), (1,)), ((), ())), preferred_element_type=F32)  185 us
    ppermute x16, waiting for transfers between devices, swap(): return lax.ppermute(value, 'dp', [(i, i ^ distance) for i in range(size)])  162 us
    dot_general x35, matrix products, dot(): return jnp.dot(a, b, preferred_element_type=F32)  141 us
    all_gather x2, waiting for transfers between devices, whole_weight(): own = lax.all_gather(own, 'tensor', axis=join, tiled=True)  93.4 us
    all_gather x2, waiting for transfers between devices, whole_weight(): return lax.all_gather(own, 'dp', axis=split, tiled=True)  86.6 us
    reduce_scatter x2, waiting for transfers between devices, sum_dp(): lax.psum_scatter(value.astype(BF16), 'tensor', scatter_dimension=scatter,...  68 us
  transfers between devices with their start and end apart: 57, of which 42 were waited for; matrix products, arithmetic and copies ran while one was open for 22% of the time, Pallas kernels for 0%

commit v1 on v0

--- a/solution.py
+++ b/solution.py
@@ -9,6 +9,22 @@
 BF16 = jnp.bfloat16
 
 
+def ring_gather(x, axis, dim):
+    ways, here, lap = (lax.axis_size(axis), lax.axis_index(axis), x.shape[dim])
+    shape = [n * ways if d == dim else n for d, n in enumerate(x.shape)]
+    full = lax.dynamic_update_slice_in_dim(jnp.zeros(shape, x.dtype), x, here * lap, axis=dim)
+    going_up = going_down = x
+    for far in range(1, ways // 2 + 1):
+        going_up = lax.ppermute(going_up, axis, [(d, (d + 1) % ways) for d in range(ways)])
+        full = lax.dynamic_update_slice_in_dim(full, going_up, (here - far) % ways * lap, axis=dim)
+        if 2 * far < ways:
+            going_down = lax.ppermute(going_down, axis, [(d, (d - 1) % ways) for d in range(ways)])
+            full = lax.dynamic_update_slice_in_dim(
+                full, going_down, (here + far) % ways * lap, axis=dim
+            )
+    return full
+
+
 def from_behind(block, axis, distance):
     devices = range(lax.axis_size(axis))
     route = [(i - distance, i) for i in devices if i - distance in devices]
@@ -39,7 +55,7 @@
 
 
 def gather_rows(own_rows):
-    return lax.all_gather(own_rows, "tensor", axis=0, tiled=True)
+    return ring_gather(own_rows, "tensor", 0)
 
 
 def sum_rows(partial):

time: 1820 us -> 1750 us (0.962)
  waiting for transfers between devices: 880 us -> 779 us
  blocking collectives: 64.5 us -> 9.28 us
  starting transfers between devices: 38.8 us -> 90.7 us
  local copies, waits for them, and re-layouts: 197 us -> 239 us
    all_gather x10 -> x0, waiting for transfers between devices: 222 us -> none  [gather_rows(): return lax.all_gather(own_rows, 'tensor', axis=0, tiled=True)]
    ppermute x0 -> x45, waiting for transfers between devices: none -> 115 us  [the longest x30 93 us: ring_gather(): lax.ppermute(going_up, axis, [(d, (d + 1) % ways) for d in range(ways)])]
    all_gather x5 -> x0, blocking collectives: 55.3 us -> none  [gather_rows(): return lax.all_gather(own_rows, 'tensor', axis=0, tiled=True)]
    ppermute x0 -> x45, starting transfers between devices: none -> 51.4 us  [the longest x15 47.8 us: ring_gather(): lax.ppermute(going_down, axis, [(d, (d - 1) % ways) for d in range(ways)])]
    dynamic_update_slice x0 -> x44, local copies, waits for them, and re-layouts: none -> 27.4 us  [the longest x29 18 us: ring_gather(): lax.dynamic_update_slice_in_dim(full, going_up, (here - far) % ways * lap...]
    reduce_scatter x15, waiting for transfers between devices: 205 us -> 225 us  [sum_rows(): lax.psum_scatter(partial.astype(BF16), 'tensor', scatter_dimension=0, til...]
    unnamed x349 -> x429, local copies, waits for them, and re-layouts: 43.3 us -> 49.1 us
    dynamic_update_slice x39 -> x40, local copies, waits for them, and re-layouts: 43.1 us -> 41.6 us  [put(): return lax.dynamic_update_index_in_dim(kept, value, index, 0)]
  transfers between devices with their start and end apart: 57 -> 92, of which waited for: 42 -> 56; matrix products, arithmetic and copies ran while one was open for 22% -> 27% of each run, Pallas kernels for 0% -> 0%
where the time goes in v1:
time: 1750 us; the launch traced here: 1740 us
  waiting for transfers between devices  779 us (45%)
  matrix products  389 us (22%)
  local copies, waits for them, and re-layouts  239 us (14%)
  other arithmetic  219 us (13%)
  starting transfers between devices  90.7 us (5%)
  between operations  18 us (1%)
    reduce_scatter x15, waiting for transfers between devices, sum_rows(): lax.psum_scatter(partial.astype(BF16), 'tensor', scatter_dimension=0, til...  225 us
    dot_general x40, matrix products, dot_t(): lax.dot_general(a, b, (((1,), (1,)), ((), ())), preferred_element_type=F32)  195 us
    ppermute x16, waiting for transfers between devices, swap(): return lax.ppermute(value, 'dp', [(i, i ^ distance) for i in range(size)])  161 us
    dot_general x35, matrix products, dot(): return jnp.dot(a, b, preferred_element_type=F32)  140 us
    all_gather x2, waiting for transfers between devices, whole_weight(): own = lax.all_gather(own, 'tensor', axis=join, tiled=True)  93.3 us
    ppermute x30, waiting for transfers between devices, ring_gather(): lax.ppermute(going_up, axis, [(d, (d + 1) % ways) for d in range(ways)])  93 us
    all_gather x2, waiting for transfers between devices, whole_weight(): return lax.all_gather(own, 'dp', axis=split, tiled=True)  89.7 us
    reduce_scatter x2, waiting for transfers between devices, sum_dp(): lax.psum_scatter(value.astype(BF16), 'tensor', scatter_dimension=scatter,...  68.3 us
  transfers between devices with their start and end apart: 92, of which 56 were waited for; matrix products, arithmetic and copies ran while one was open for 27% of the time, Pallas kernels for 0%

profile of v1, /device:TPU:1, one launch (start us, length us, event | category | flops | bytes accessed | tf_op | source)
XLA Modules:
  0.0 1743.7 jit_solution(18040095591800715280)
XLA Ops:
  11.7 46.5 %all-gather.10.cloned.1.call-done = bf16[1,512,2048]{2,1,0:T(8,128)(2,1)} async-done(((bf16[1,512,512]{2,1,0:T(8,128)(2,1)}), bf16[1,512,2048]{2,1,0:T(8,128)(2,1)}) %all-gather.10.cloned.1.call-update) | async-done | bytes 2097168 | tf_op jit(solution)/shard_map/all_gather | solution.py:109
  58.3 46.8 %all-gather.14.cloned.1.call-done = bf16[1,2048,512]{2,1,0:T(8,128)(2,1)} async-done(((bf16[1,512,512]{2,1,0:T(8,128)(2,1)}), bf16[1,2048,512]{2,1,0:T(8,128)(2,1)}) %all-gather.14.cloned.1.call-update) | async-done | bytes 2097168 | tf_op jit(solution)/shard_map/all_gather | solution.py:109
  109.4 9.3 all-gather.2
  123.5 40.6 %all-gather.12.cloned.1.call-done = bf16[1,2048,2048]{2,1,0:T(8,128)(2,1)} async-done(((bf16[1,512,2048]{2,1,0:T(8,128)(2,1)}), bf16[1,2048,2048]{2,1,0:T(8,128)(2,1)}) %all-gather.12.cloned.1.call-update) | async-done | bytes 8388624 | tf_op jit(solution)/shard_map/all_gather | solution.py:110
  174.8 49.1 %all-gather.16.cloned.1.call-done = bf16[1,2048,2048]{2,1,0:T(8,128)(2,1)} async-done(((bf16[1,2048,512]{2,1,0:T(8,128)(2,1)}), bf16[1,2048,2048]{2,1,0:T(8,128)(2,1)}) %all-gather.16.cloned.1.call-update) | async-done | bytes 8388624 | tf_op jit(solution)/shard_map/all_gather | solution.py:110
  254.5 7.2 bitcast_dynamic-update-slice_fusion.4
  266.7 25.9 %reduce-scatter.18.cloned.1.call-done = bf16[64,2048]{1,0:T(8,128)(2,1)} async-done(((bf16[256,2048]{1,0:T(8,128)(2,1)}), bf16[64,2048]{1,0:T(8,128)(2,1)}) %reduce-scatter.18.cloned.1.call-update) | async-done | bytes 262160 | tf_op jit(solution)/shard_map/reduce_scatter | solution.py:62
  341.2 7.1 collective-permute-done.12
  348.4 7.5 bitcast_dynamic-update-slice_fusion.3
  360.8 31.2 %reduce-scatter.20.cloned.1.call-done = bf16[64,2048]{1,0:T(8,128)(2,1)} async-done(((bf16[256,2048]{1,0:T(8,128)(2,1)}), bf16[64,2048]{1,0:T(8,128)(2,1)}) %reduce-scatter.20.cloned.1.call-update) | async-done | bytes 262160 | tf_op jit(solution)/shard_map/reduce_scatter | solution.py:62
  436.2 7.2 collective-permute-done.19
  443.5 7.5 bitcast_dynamic-update-slice_fusion.2
  465.6 30.5 %reduce-scatter.22.cloned.1.call-done = bf16[64,2048]{1,0:T(8,128)(2,1)} async-done(((bf16[256,2048]{1,0:T(8,128)(2,1)}), bf16[64,2048]{1,0:T(8,128)(2,1)}) %reduce-scatter.22.cloned.1.call-update) | async-done | bytes 262160 | tf_op jit(solution)/shard_map/reduce_scatter | solution.py:62
  561.6 7.4 bitcast_dynamic-update-slice_fusion.1
  570.4 6.9 fusion.132
  583.3 24.6 %reduce-scatter.24.cloned.1.call-done = bf16[64,2048]{1,0:T(8,128)(2,1)} async-done(((bf16[256,2048]{1,0:T(8,128)(2,1)}), bf16[64,2048]{1,0:T(8,128)(2,1)}) %reduce-scatter.24.cloned.1.call-update) | async-done | bytes 262160 | tf_op jit(solution)/shard_map/reduce_scatter | solution.py:62
  673.4 8.5 bitcast_dynamic-update-slice_fusion
  703.8 19.0 %reduce-scatter.28.cloned.1.call-done = bf16[64,2048]{1,0:T(8,128)(2,1)} async-done(((bf16[256,2048]{1,0:T(8,128)(2,1)}), bf16[64,2048]{1,0:T(8,128)(2,1)}) %reduce-scatter.28.cloned.1.call-update) | async-done | bytes 262160 | tf_op jit(solution)/shard_map/reduce_scatter | solution.py:62
  752.9 6.9 fusion.68
  759.8 8.9 reduce-scatter.30.cloned.1.call-done
  803.9 8.6 bitcast_dynamic-update-slice_fusion.13
  827.0 21.7 %reduce-scatter.32.cloned.1.call-done = bf16[64,2048]{1,0:T(8,128)(2,1)} async-done(((bf16[256,2048]{1,0:T(8,128)(2,1)}), bf16[64,2048]{1,0:T(8,128)(2,1)}) %reduce-scatter.32.cloned.1.call-update) | async-done | bytes 262160 | tf_op jit(solution)/shard_map/reduce_scatter | solution.py:62
  879.1 6.9 fusion.66
  886.1 8.8 reduce-scatter.34.cloned.1.call-done
  931.9 8.7 bitcast_dynamic-update-slice_fusion.12
  963.9 14.5 reduce-scatter.36.cloned.1.call-done
  1007.8 6.8 fusion.64
  1014.6 8.8 reduce-scatter.38.cloned.1.call-done
  1058.1 8.6 bitcast_dynamic-update-slice_fusion.11
  1089.5 13.8 reduce-scatter.40.cloned.1.call-done
  1133.5 6.8 fusion.62
  1140.3 8.6 reduce-scatter.42.cloned.1.call-done
  1176.9 7.6 collective-permute-done.52
  1185.2 8.6 bitcast_dynamic-update-slice_fusion.10
  1211.5 7.6 fusion.135
  1219.2 9.0 reduce-scatter.44.cloned.1.call-done
  1274.6 15.6 convolution_bitcast_fusion.1
  1331.9 8.4 add_convert_fusion.1
  1340.4 12.5 convolution_bitcast_fusion
  1396.1 40.2 %collective-permute-done.62 = bf16[512,2048]{1,0:T(8,128)(2,1)} collective-permute-done((bf16[512,2048]{1,0:T(8,128)(2,1)S(1)}, bf16[512,2048]{1,0:T(8,128)(2,1)}, u32[]{:S(2)}, u32[]{:S(2)}) %collective-permute-start.62) | collective-permute-done | bytes 2097184 | tf_op jit(solution)/shard_map/ppermute | solution.py:69
  1441.5 8.3 add_convert_fusion
  1452.6 31.0 %collective-permute-done.66 = bf16[512,2048]{1,0:T(8,128)(2,1)} collective-permute-done((bf16[512,2048]{1,0:T(8,128)(2,1)}, bf16[512,2048]{1,0:T(8,128)(2,1)}, u32[]{:S(2)}, u32[]{:S(2)}) %collective-permute-start.66) | collective-permute-done | bytes 2097184 | tf_op jit(solution)/shard_map/ppermute | solution.py:69
  1488.4 43.0 %collective-permute-done.63 = bf16[512,2048]{1,0:T(8,128)(2,1)} collective-permute-done((bf16[512,2048]{1,0:T(8,128)(2,1)S(1)}, bf16[512,2048]{1,0:T(8,128)(2,1)}, u32[]{:S(2)}, u32[]{:S(2)}) %collective-permute-start.63) | collective-permute-done | bytes 2097184 | tf_op jit(solution)/shard_map/ppermute | solution.py:69
  1539.9 36.4 %collective-permute-done.67 = bf16[512,2048]{1,0:T(8,128)(2,1)S(1)} collective-permute-done((bf16[512,2048]{1,0:T(8,128)(2,1)S(1)}, bf16[512,2048]{1,0:T(8,128)(2,1)S(1)}, u32[]{:S(2)}, u32[]{:S(2)}) %collective-permute-start.67) | collective-permute-done | bytes 2097184 | tf_op jit(solution)/shard_map/ppermute | solution.py:69
  1603.0 68.3 %reduce-scatter.50.cloned.1.call-done = bf16[512,1024]{1,0:T(8,128)(2,1)} async-done(((bf16[2048,1024]{1,0:T(8,128)(2,1)}), bf16[512,1024]{1,0:T(8,128)(2,1)}) %reduce-scatter.50.cloned.1.call-update) | async-done | bytes 1048592 | tf_op jit(solution)/shard_map/reduce_scatter | solution.py:94
  1676.2 11.8 maximum_convert_fusion
  1705.6 7.8 collective-permute-done.59
  1716.4 11.8 maximum_convert_fusion.1
  (1082 shorter events, 876.3 us)
Async XLA Ops:
  7.2 51.0 %all-gather.10.cloned.1.call-start = ((), (), s32[]{:S(2)}) async-start(), calls=%async_computation.36 | async-start | bytes 2621440 | tf_op jit(solution)/shard_map/all_gather | solution.py:109
  9.7 95.4 %all-gather.14.cloned.1.call-start = ((), (), s32[]{:S(2)}) async-start(), calls=%async_computation.38 | async-start | bytes 2621440 | tf_op jit(solution)/shard_map/all_gather | solution.py:109
  11.7 152.4 %all-gather.12.cloned.1.call-start = ((), (), s32[]{:S(2)}) async-start(), calls=%async_computation.37 | async-start | bytes 10485760 | tf_op jit(solution)/shard_map/all_gather | solution.py:110
  58.3 165.6 %all-gather.16.cloned.1.call-start = ((), (), s32[]{:S(2)}) async-start(), calls=%async_computation.39 | async-start | bytes 10485760 | tf_op jit(solution)/shard_map/all_gather | solution.py:110
  105.1 187.5 %reduce-scatter.18.cloned.1.call-start = ((), (), s32[]{:S(2)}) async-start(), calls=%async_computation.17 | async-start | bytes 1310720 | tf_op jit(solution)/shard_map/reduce_scatter | solution.py:62
  106.1 12.7 collective-permute-start
  106.2 12.7 collective-permute-start.1
  230.8 13.3 collective-permute-start.4
  266.6 125.4 %reduce-scatter.20.cloned.1.call-start = ((), (), s32[]{:S(2)}) async-start(), calls=%async_computation.18 | async-start | bytes 1310720 | tf_op jit(solution)/shard_map/reduce_scatter | solution.py:62
  360.7 135.3 %reduce-scatter.22.cloned.1.call-start = ((), (), s32[]{:S(2)}) async-start(), calls=%async_computation.19 | async-start | bytes 1310720 | tf_op jit(solution)/shard_map/reduce_scatter | solution.py:62
  455.8 152.1 %reduce-scatter.24.cloned.1.call-start = ((), (), s32[]{:S(2)}) async-start(), calls=%async_computation.20 | async-start | bytes 1310720 | tf_op jit(solution)/shard_map/reduce_scatter | solution.py:62
  464.5 201.5 %collective-permute-start.36 = (bf16[64,2048]{1,0:T(8,128)(2,1)}, bf16[64,2048]{1,0:T(8,128)(2,1)}, u32[]{:S(2)}, u32[]{:S(2)}) collective-permute-start(bf16[64,2048]{1,0:T(8,128)(2,1)} %collective-permute-done.34), channel_id=1, source_target_pairs={{0,4},{4,8},{8,12},{12,0},{1,5},{5,9},{9,13},{13,1},{2,6},{6,10},{... | collective-permute-start | bytes 786440 | tf_op jit(solution)/shard_map/ppermute | solution.py:18
  510.3 11.9 collective-permute-start.22
  543.8 14.4 collective-permute-start.25
  577.3 145.5 %reduce-scatter.28.cloned.1.call-start = ((), (), s32[]{:S(2)}) async-start(), calls=%async_computation.22 | async-start | bytes 1310720 | tf_op jit(solution)/shard_map/reduce_scatter | solution.py:62
  621.0 12.5 collective-permute-start.29
  659.9 12.4 collective-permute-start.33
  694.4 74.2 %reduce-scatter.30.cloned.1.call-start = ((), (), s32[]{:S(2)}) async-start(), calls=%async_computation.23 | async-start | bytes 163840 | tf_op jit(solution)/shard_map/reduce_scatter | solution.py:62
  752.8 95.9 %reduce-scatter.32.cloned.1.call-start = ((), (), s32[]{:S(2)}) async-start(), calls=%async_computation.24 | async-start | bytes 1310720 | tf_op jit(solution)/shard_map/reduce_scatter | solution.py:62
  819.4 75.6 %reduce-scatter.34.cloned.1.call-start = ((), (), s32[]{:S(2)}) async-start(), calls=%async_computation.25 | async-start | bytes 163840 | tf_op jit(solution)/shard_map/reduce_scatter | solution.py:62
  879.1 99.3 %reduce-scatter.36.cloned.1.call-start = ((), (), s32[]{:S(2)}) async-start(), calls=%async_computation.26 | async-start | bytes 1310720 | tf_op jit(solution)/shard_map/reduce_scatter | solution.py:62
  911.0 12.9 collective-permute-start.42
  947.3 76.2 %reduce-scatter.38.cloned.1.call-start = ((), (), s32[]{:S(2)}) async-start(), calls=%async_computation.27 | async-start | bytes 163840 | tf_op jit(solution)/shard_map/reduce_scatter | solution.py:62
  1007.6 95.7 %reduce-scatter.40.cloned.1.call-start = ((), (), s32[]{:S(2)}) async-start(), calls=%async_computation.28 | async-start | bytes 1310720 | tf_op jit(solution)/shard_map/reduce_scatter | solution.py:62
  1073.5 75.4 %reduce-scatter.42.cloned.1.call-start = ((), (), s32[]{:S(2)}) async-start(), calls=%async_computation.29 | async-start | bytes 163840 | tf_op jit(solution)/shard_map/reduce_scatter | solution.py:62
  1133.0 95.1 %reduce-scatter.44.cloned.1.call-start = ((), (), s32[]{:S(2)}) async-start(), calls=%async_computation.30 | async-start | bytes 1310720 | tf_op jit(solution)/shard_map/reduce_scatter | solution.py:62
  1200.6 123.6 %reduce-scatter.46.cloned.1.call-start = ((), (), s32[]{:S(2)}) async-start(), calls=%async_computation.31 | async-start | bytes 163840 | tf_op jit(solution)/shard_map/reduce_scatter | solution.py:62
  1250.7 199.2 %reduce-scatter.26.cloned.1.call-start = ((), (), s32[]{:S(2)}) async-start(), calls=%async_computation.21 | async-start | bytes 1310720 | tf_op jit(solution)/shard_map/reduce_scatter | solution.py:62
  1254.9 330.5 %all-reduce.4.cloned.1.call-start = ((), (), s32[]{:S(2)}) async-start(), calls=%async_computation.32 | async-start | bytes 188416 | tf_op jit(solution)/shard_map/psum | solution.py:302
  1304.7 27.3 %collective-permute-start.53 = (bf16[1024,2048]{1,0:T(8,128)(2,1)}, bf16[1024,2048]{1,0:T(8,128)(2,1)}, u32[]{:S(2)}, u32[]{:S(2)}) collective-permute-start(bf16[1024,2048]{1,0:T(8,128)(2,1)} %dynamic-slice_convert_fusion.3), channel_id=1, source_target_pairs={{0,1},{1,0},{2,3},{3,2},{4,5},{5,4},{6,7},{7,6},{8,9},{9,8},{10,11... | collective-permute-start | bytes 12582920 | tf_op jit(solution)/shard_map/ppermute | solution.py:69
  1314.9 62.1 %collective-permute-start.61 = (bf16[1024,2048]{1,0:T(8,128)(2,1)}, bf16[1024,2048]{1,0:T(8,128)(2,1)}, u32[]{:S(2)}, u32[]{:S(2)}) collective-permute-start(bf16[1024,2048]{1,0:T(8,128)(2,1)} %dynamic-slice_convert_fusion.1), channel_id=1, source_target_pairs={{0,1},{1,0},{2,3},{3,2},{4,5},{5,4},{6,7},{7,6},{8,9},{9,8},{10,11... | collective-permute-start | bytes 12582920 | tf_op jit(solution)/shard_map/ppermute | solution.py:69
  1329.0 260.4 %all-reduce.6.cloned.1.call-start = ((), (), s32[]{:S(2)}) async-start(), calls=%async_computation.34 | async-start | bytes 2097152 | tf_op jit(solution)/shard_map/psum | solution.py:298
  1331.9 267.0 %reduce-scatter.48.cloned.1.call-start = ((), (), s32[]{:S(2)}) async-start(), calls=%async_computation.33 | async-start | bytes 5242880 | tf_op jit(solution)/shard_map/reduce_scatter | solution.py:94
  1340.4 330.9 %reduce-scatter.50.cloned.1.call-start = ((), (), s32[]{:S(2)}) async-start(), calls=%async_computation.35 | async-start | bytes 5242880 | tf_op jit(solution)/shard_map/reduce_scatter | solution.py:94
  1361.3 26.7 %collective-permute-start.65 = (bf16[1024,2048]{1,0:T(8,128)(2,1)}, bf16[1024,2048]{1,0:T(8,128)(2,1)}, u32[]{:S(2)}, u32[]{:S(2)}) collective-permute-start(bf16[1024,2048]{1,0:T(8,128)(2,1)} %dynamic-slice_convert_fusion), channel_id=1, source_target_pairs={{0,1},{1,0},{2,3},{3,2},{4,5},{5,4},{6,7},{7,6},{8,9},{9,8},{10,11... | collective-permute-start | bytes 12582920 | tf_op jit(solution)/shard_map/ppermute | solution.py:69
  1377.0 64.5 %collective-permute-start.57 = (bf16[2048,1024]{1,0:T(8,128)(2,1)}, bf16[2048,1024]{1,0:T(8,128)(2,1)}, u32[]{:S(2)}, u32[]{:S(2)}) collective-permute-start(bf16[2048,1024]{1,0:T(8,128)(2,1)} %dynamic-slice_convert_fusion.2), channel_id=1, source_target_pairs={{0,1},{1,0},{2,3},{3,2},{4,5},{5,4},{6,7},{7,6},{8,9},{9,8},{10,11... | collective-permute-start | bytes 12582920 | tf_op jit(solution)/shard_map/ppermute | solution.py:69
  1386.7 49.7 %collective-permute-start.62 = (bf16[512,2048]{1,0:T(8,128)(2,1)S(1)}, bf16[512,2048]{1,0:T(8,128)(2,1)}, u32[]{:S(2)}, u32[]{:S(2)}) collective-permute-start(bf16[512,2048]{1,0:T(8,128)(2,1)S(1)} %dynamic-slice_convert_fusion.5), channel_id=1, source_target_pairs={{0,2},{1,3},{2,0},{3,1},{4,6},{5,7},{6,4},{7,5},{8,10},{9,11},{10,... | collective-permute-start | bytes 6291464 | tf_op jit(solution)/shard_map/ppermute | solution.py:69
  1396.0 87.6 %collective-permute-start.66 = (bf16[512,2048]{1,0:T(8,128)(2,1)}, bf16[512,2048]{1,0:T(8,128)(2,1)}, u32[]{:S(2)}, u32[]{:S(2)}) collective-permute-start(bf16[512,2048]{1,0:T(8,128)(2,1)} %dynamic-slice_convert_fusion.4), channel_id=1, source_target_pairs={{0,2},{1,3},{2,0},{3,1},{4,6},{5,7},{6,4},{7,5},{8,10},{9,11},{10,... | collective-permute-start | bytes 6291464 | tf_op jit(solution)/shard_map/ppermute | solution.py:69
  1439.9 91.5 %collective-permute-start.63 = (bf16[512,2048]{1,0:T(8,128)(2,1)S(1)}, bf16[512,2048]{1,0:T(8,128)(2,1)}, u32[]{:S(2)}, u32[]{:S(2)}) collective-permute-start(bf16[512,2048]{1,0:T(8,128)(2,1)S(1)} %add_convert_fusion.3), channel_id=1, source_target_pairs={{0,2},{1,3},{2,0},{3,1},{4,6},{5,7},{6,4},{7,5},{8,10},{9,11},{10,... | collective-permute-start | bytes 6291464 | tf_op jit(solution)/shard_map/ppermute | solution.py:69
  1487.1 89.2 %collective-permute-start.67 = (bf16[512,2048]{1,0:T(8,128)(2,1)S(1)}, bf16[512,2048]{1,0:T(8,128)(2,1)S(1)}, u32[]{:S(2)}, u32[]{:S(2)}) collective-permute-start(bf16[512,2048]{1,0:T(8,128)(2,1)S(1)} %add_convert_fusion.2), channel_id=1, source_target_pairs={{0,2},{1,3},{2,0},{3,1},{4,6},{5,7},{6,4},{7,5},{8,10},{9,11},{10,... | collective-permute-start | bytes 6291464 | tf_op jit(solution)/shard_map/ppermute | solution.py:69
  1536.8 55.5 %collective-permute-start.64 = (bf16[1024,2048]{1,0:T(8,128)(2,1)}, bf16[1024,2048]{1,0:T(8,128)(2,1)}, u32[]{:S(2)}, u32[]{:S(2)}) collective-permute-start(bf16[1024,2048]{1,0:T(8,128)(2,1)} %pad_maximum_fusion), channel_id=1, source_target_pairs={{0,1},{1,0},{2,3},{3,2},{4,5},{5,4},{6,7},{7,6},{8,9},{9,8},{10,11... | collective-permute-start | bytes 12582920 | tf_op jit(solution)/shard_map/ppermute | solution.py:69
  1579.6 113.1 %collective-permute-start.68 = (bf16[1024,2048]{1,0:T(8,128)(2,1)}, bf16[1024,2048]{1,0:T(8,128)(2,1)}, u32[]{:S(2)}, u32[]{:S(2)}) collective-permute-start(bf16[1024,2048]{1,0:T(8,128)(2,1)} %pad_maximum_fusion.1), channel_id=1, source_target_pairs={{0,1},{1,0},{2,3},{3,2},{4,5},{5,4},{6,7},{7,6},{8,9},{9,8},{10,11... | collective-permute-start | bytes 12582920 | tf_op jit(solution)/shard_map/ppermute | solution.py:69
  1601.7 86.3 %collective-permute-start.54 = (bf16[512,512]{1,0:T(8,128)(2,1)S(1)}, bf16[512,512]{1,0:T(8,128)(2,1)S(1)}, u32[]{:S(2)}, u32[]{:S(2)}) collective-permute-start(bf16[512,512]{1,0:T(8,128)(2,1)S(1)} %dynamic-slice_convert_fusion.7), channel_id=1, source_target_pairs={{0,2},{1,3},{2,0},{3,1},{4,6},{5,7},{6,4},{7,5},{8,10},{9,11},{10,... | collective-permute-start | bytes 1572872 | tf_op jit(solution)/shard_map/ppermute | solution.py:69
  1675.0 14.9 collective-permute-start.58
  1689.5 12.6 collective-permute-start.55
  1691.4 21.9 %collective-permute-start.59 = (bf16[512,512]{1,0:T(8,128)(2,1)S(1)}, bf16[512,512]{1,0:T(8,128)(2,1)S(1)}, u32[]{:S(2)}, u32[]{:S(2)}) collective-permute-start(bf16[512,512]{1,0:T(8,128)(2,1)S(1)} %add_convert_fusion.4), channel_id=1, source_target_pairs={{0,2},{1,3},{2,0},{3,1},{4,6},{5,7},{6,4},{7,5},{8,10},{9,11},{10,... | collective-permute-start | bytes 1572872 | tf_op jit(solution)/shard_map/ppermute | solution.py:69
  1702.3 25.9 %collective-permute-start.56 = (bf16[1024,512]{1,0:T(8,128)(2,1)S(1)}, bf16[1024,512]{1,0:T(8,128)(2,1)}, u32[]{:S(2)}, u32[]{:S(2)}) collective-permute-start(bf16[1024,512]{1,0:T(8,128)(2,1)S(1)} %pad_maximum_fusion.3), channel_id=1, source_target_pairs={{0,1},{1,0},{2,3},{3,2},{4,5},{5,4},{6,7},{7,6},{8,9},{9,8},{10,11... | collective-permute-start | bytes 3145736 | tf_op jit(solution)/shard_map/ppermute | solution.py:69
  1714.6 17.9 %collective-permute-start.60 = (bf16[512,1024]{1,0:T(8,128)(2,1)}, bf16[512,1024]{1,0:T(8,128)(2,1)}, u32[]{:S(2)}, u32[]{:S(2)}) collective-permute-start(bf16[512,1024]{1,0:T(8,128)(2,1)} %pad_maximum_fusion.4), channel_id=1, source_target_pairs={{0,1},{1,0},{2,3},{3,2},{4,5},{5,4},{6,7},{7,6},{8,9},{9,8},{10,11... | collective-permute-start | bytes 3145736 | tf_op jit(solution)/shard_map/ppermute | solution.py:69
  (257 other events, 4176.9 us)
Sparse Core Ops, SparseCore 0:
  10.2 47.9 all-gather.9
  60.4 44.6 all-gather.13
  106.7 57.4 all-gather.11
  165.5 58.2 all-gather.15
  266.7 25.8 reduce-scatter.17
  360.9 31.0 reduce-scatter.19
  455.9 40.0 reduce-scatter.21
  577.4 30.4 reduce-scatter.23
  694.6 28.2 reduce-scatter.27
  752.9 15.6 reduce-scatter.29
  819.5 29.1 reduce-scatter.31
  879.2 15.6 reduce-scatter.33
  947.4 30.9 reduce-scatter.35
  1007.7 15.6 reduce-scatter.37
  1073.6 29.6 reduce-scatter.39
  1133.2 15.7 reduce-scatter.41
  1200.8 27.3 reduce-scatter.43
  1250.8 15.7 reduce-scatter.45
  1268.9 27.4 reduce-scatter.25
  1329.2 85.1 all-reduce.3
  1417.8 93.6 all-reduce.5
  1514.3 76.5 reduce-scatter.47
  1594.0 77.2 reduce-scatter.49
